TPU v7x, 256 devices: a whole 4x4x8 slice. The times are simulated.
256 devices in a mesh: row: 16 (over z, y_lo), col: 16 (over x, y_hi, core).
Axes of the slice: x: 4, y: 4 (y_hi: 2, y_lo: 2; y = y_hi * 2 + y_lo), z: 8, core: 2. Of those that a mesh axis runs over, the one named last changes fastest.
Arguments:
- raw: int32 [32768, 4096], P('col', 'row'), may hold values from -128 to 127
- taps: int32 [16, 128], replicated, may hold values from -256 to 256
Outputs:
- visibility: bfloat16 [32, 4096, 2, 4096], P(None, 'row', None, 'col')
All inputs are finite; a program needn't handle non-finite values.
Results may differ from a plain program's by a relative error of at most 0.0056.
Values may be sent and summed in bfloat16 or wider, within the bound.
A program may use at most 128 MiB of HBM per device.

v0:
```python
import math
import jax
import jax.numpy as jnp
from jax import lax
from jax.sharding import PartitionSpec as P

CHANNELS = 32
TRANSFORM = 128
TAPS = 16
SPECTRA_DEV = 16
BLOCKS = 2


def from_behind(block, axis, distance):
    devices = range(lax.axis_size(axis))
    route = [(i - distance, i) for i in devices if i - distance in devices]
    return lax.ppermute(block, axis, route)


def from_root(value, axis, root):
    mine = lax.axis_index(axis) == root
    return lax.psum(jnp.where(mine, value, jnp.zeros_like(value)), axis)


def dft_table():
    sample = jnp.arange(TRANSFORM, dtype=jnp.int32)[:, None]
    channel = jnp.arange(1, CHANNELS + 1, dtype=jnp.int32)[None, :]
    phase = (sample * channel % TRANSFORM).astype(jnp.float32) * (2.0 * math.pi / TRANSFORM)
    return jnp.concatenate([jnp.cos(phase), -jnp.sin(phase)], axis=1)


def channelize(extended, taps, count):
    coeffs = taps.astype(jnp.float32)
    weighted = jnp.zeros((count, TRANSFORM, extended.shape[2]), jnp.float32)
    for offset in range(TAPS):
        start = TAPS - 1 - offset
        weighted = weighted + coeffs[offset][None, :, None] * extended[
            start : start + count
        ].astype(jnp.float32)
    scale = 1.0 / (8192.0 * math.sqrt(TAPS * TRANSFORM))
    spectra = (
        jnp.einsum("sni,nk->ksi", weighted, dft_table(), precision=lax.Precision.HIGHEST) * scale
    )
    return spectra.reshape(2, CHANNELS, count, extended.shape[2]).astype(jnp.bfloat16)


def correlate(row_block, column_block):
    spectra_all = row_block.shape[2]
    width = spectra_all // BLOCKS
    total = None
    for block in range(BLOCKS):
        left = jnp.concatenate(
            [
                row_block[0, :, block * width : (block + 1) * width],
                row_block[1, :, block * width : (block + 1) * width],
            ],
            axis=1,
        )
        real_part = column_block[0, :, block * width : (block + 1) * width]
        imag_part = column_block[1, :, block * width : (block + 1) * width]
        right = jnp.concatenate(
            [
                jnp.concatenate([real_part, imag_part], axis=1),
                jnp.concatenate([-imag_part, real_part], axis=1),
            ],
            axis=2,
        )
        term = lax.dot_general(
            left, right, (((1,), (1,)), ((0,), (0,))), preferred_element_type=jnp.float32
        )
        if block == 0:
            total = term
        else:
            summed = total + term
            total = summed
    result = (total * (1.0 / spectra_all)).astype(jnp.bfloat16)
    return result.reshape(CHANNELS, row_block.shape[3], 2, column_block.shape[3])


def body(raw, taps):
    frames = raw.astype(jnp.bfloat16).reshape(SPECTRA_DEV, TRANSFORM, raw.shape[1])
    rim_frames = frames[SPECTRA_DEV - (TAPS - 1) :]
    earlier = from_behind(rim_frames, "col", 1)
    extended = jnp.concatenate([earlier, frames], axis=0)
    pieces = channelize(extended, taps, SPECTRA_DEV)
    row_block = lax.all_gather(pieces, "col", axis=2, tiled=True)
    ratio = lax.axis_size("row") // lax.axis_size("col")
    first_root = lax.axis_index("col") * ratio
    received = from_root(row_block, "row", first_root + 0)
    return correlate(row_block, received)


def solution(mesh):
    placed = (P("col", "row"), P())
    return jax.shard_map(
        body, mesh=mesh, in_specs=placed, out_specs=P(None, "row", None, "col"), check_vma=False
    )
```

profile of v0, /device:TPU:1, one launch (start us, length us, event | category | flops | bytes accessed | tf_op | source)
XLA Modules:
  0.0 541.9 jit_solution(9237460583808072064)
XLA Ops:
  6.5 0.0 copy-start.1
  6.5 0.0 all-gather.2.cloned.1.call-start
  6.5 1.8 convert_element_type.70
  8.3 0.1 slice.166
  8.4 6.2 %collective-permute-start = (bf16[15,128,256]{2,1,0:T(8,128)(2,1)S(1)}, bf16[15,128,256]{2,1,0:T(8,128)(2,1)S(1)}, u32[]{:S(2)}, u32[]{:S(2)}) collective-permute-start(bf16[15,128,256]{2,1,0:T(8,128)(2,1)S(1)} %bitcast.59), channel_id=1, source_target_pairs={{0,1},{1,2},{2,3},{3,4},{4,5},{5,6},{6,7},{7,8},{8,9},{9,10},{10,1... | collective-permute-start | bytes 2949128 | tf_op jit(solution)/shard_map/ppermute | solution.py:17
  14.6 0.0 copy-done.1
  14.7 0.2 fusion.128
  14.8 10.8 %collective-permute-done = bf16[15,128,256]{2,1,0:T(8,128)(2,1)S(1)} collective-permute-done((bf16[15,128,256]{2,1,0:T(8,128)(2,1)S(1)}, bf16[15,128,256]{2,1,0:T(8,128)(2,1)S(1)}, u32[]{:S(2)}, u32[]{:S(2)}) %collective-permute-start) | collective-permute-done | bytes 983072 | tf_op jit(solution)/shard_map/ppermute | solution.py:17
  25.6 5.2 fusion.72
  30.8 1.1 copy.3
  31.9 0.0 all-gather.2.cloned.1.call-update
  31.9 0.0 all-reduce.2.cloned.1.call-start
  32.0 89.2 %all-gather.2.cloned.1.call-done = bf16[2,32,256,256]{3,2,1,0:T(8,128)(2,1)} async-done(((bf16[2,32,16,256]{3,2,1,0:T(8,128)(2,1)}), bf16[2,32,256,256]{3,2,1,0:T(8,128)(2,1)}) %all-gather.2.cloned.1.call-update) | async-done | bytes 8388624 | tf_op jit(solution)/shard_map/all_gather | solution.py:86
  121.2 3.9 broadcast_select_fusion
  125.1 0.0 all-reduce.2.cloned.1.call-update
  125.1 5.6 %slice_bitcast_fusion.3 = (bf16[32,128,256]{2,1,0:T(8,128)(2,1)S(1)}, bf16[32,128,256]{2,1,0:T(8,128)(2,1)}, bf16[32,128,256]{2,1,0:T(8,128)(2,1)}, bf16[32,128,256]{2,1,0:T(8,128)(2,1)}) fusion(bf16[2,32,256,256]{3,2,1,0:T(8,128)(2,1)} %all-gather.2.cloned.1.call-done), kind=kLoop, calls=%fused_computation.54 | loop fusion | bytes 16777216 | tf_op jit(solution)/shard_map/squeeze | solution.py:54
  130.8 361.4 %all-reduce.2.cloned.1.call-done = bf16[2,32,256,256]{3,2,1,0:T(8,128)(2,1)} async-done(((bf16[2,32,256,256]{3,2,1,0:T(8,128)(2,1)}), bf16[2,32,256,256]{3,2,1,0:T(8,128)(2,1)}) %all-reduce.2.cloned.1.call-update) | async-done | bytes 8388624 | tf_op jit(solution)/shard_map/psum | solution.py:22
  492.2 0.0 copy-start
  492.2 2.6 fusion.134
  494.8 2.0 copy-done
  496.8 3.4 slice_bitcast_fusion
  500.3 10.2 %fusion = f32[32,256,512]{2,1,0:T(8,128)} fusion(bf16[32,128,256]{2,1,0:T(8,128)(2,1)} %get-tuple-element.12, bf16[32,128,256]{2,1,0:T(8,128)(2,1)S(1)} %get-tuple-element.14, bf16[32,128,256]{2,1,0:T(8,128)(2,1)} %get-tuple-element.11, bf16[32,128,256]{2,1,0:T(8,128)(2,1)} %get-tuple-element.7, bf16[32,128,256]{2,1,0:T(8,128)(2,1)} %get-tuple-element.8), kind=kOutput, calls=%fused_computation.1 | convolution fusion | flops 2189426688 | bytes 27262976 | tf_op jit(solution)/shard_map/dot_general | solution.py:68
  510.5 12.1 %multiply_convert_fusion = bf16[32,256,512]{2,1,0:T(8,128)(2,1)} fusion(f32[32,256,512]{2,1,0:T(8,128)} %fusion, bf16[32,128,256]{2,1,0:T(8,128)(2,1)} %get-tuple-element.10, bf16[32,128,256]{2,1,0:T(8,128)(2,1)S(1)} %get-tuple-element.13, bf16[32,128,256]{2,1,0:T(8,128)(2,1)} %get-tuple-element.9, bf16[32,128,256]{2,1,0:T(8,128)(2,1)} %get-tuple-element.6, ...), kind=kOutput, calls=%fused_computation | convolution fusion | flops 2202009600 | bytes 35651584 | tf_op jit(solution)/shard_map/dot_general | solution.py:68
  522.6 12.5 %reshape.30 = bf16[32,256,2,256]{3,2,1,0:T(2,128)(2,1)} reshape(bf16[32,256,512]{2,1,0:T(8,128)(2,1)} %multiply_convert_fusion) | data formatting | bytes 16777216 | tf_op jit(solution)/shard_map/reshape | solution.py:77
  (3 shorter events, 0.0 us)
Async XLA Ops:
  6.5 8.1 %copy-start.1 = (s32[16,128]{1,0:T(8,128)S(1)}, s32[16,128]{1,0:T(8,128)}, u32[]{:S(2)}) copy-start(s32[16,128]{1,0:T(8,128)} %param.3) | copy-start | bytes 24580
  6.5 114.6 %all-gather.2.cloned.1.call-start = ((), (), s32[]{:S(2)}) async-start(), calls=%async_computation | async-start | bytes 8912896 | tf_op jit(solution)/shard_map/all_gather | solution.py:86
  8.4 17.2 %collective-permute-start = (bf16[15,128,256]{2,1,0:T(8,128)(2,1)S(1)}, bf16[15,128,256]{2,1,0:T(8,128)(2,1)S(1)}, u32[]{:S(2)}, u32[]{:S(2)}) collective-permute-start(bf16[15,128,256]{2,1,0:T(8,128)(2,1)S(1)} %bitcast.59), channel_id=1, source_target_pairs={{0,1},{1,2},{2,3},{3,4},{4,5},{5,6},{6,7},{7,8},{8,9},{9,10},{10,1... | collective-permute-start | bytes 2949128 | tf_op jit(solution)/shard_map/ppermute | solution.py:17
  31.9 460.3 %all-reduce.2.cloned.1.call-start = ((), (), s32[]{:S(2)}) async-start(), calls=%async_computation.1 | async-start | bytes 16777216 | tf_op jit(solution)/shard_map/psum | solution.py:22
  492.2 4.6 copy-start
Sparse Core Ops, SparseCore 0:
  32.0 89.1 all-gather.1
  125.3 366.8 all-reduce.1
where the time goes:
time: 542 us
  waiting for transfers between devices  461 us (85%)
  matrix products  27.5 us (5%)
  local copies, waits for them, and re-layouts  24.7 us (5%)
  between operations  13.5 us (2%)
  other arithmetic  8.52 us (2%)
  starting transfers between devices  6.26 us (1%)
    psum x1, waiting for transfers between devices, from_root(): return lax.psum(jnp.where(mine, value, jnp.zeros_like(value)), axis)  361 us
    all_gather x1, waiting for transfers between devices, body(): row_block = lax.all_gather(pieces, 'col', axis=2, tiled=True)  89.2 us
    dot_general x2, matrix products, correlate(): lax.dot_general(left, right, (((1,), (1,)), ((0,), (0,))), preferred_elem...  22.3 us
    reshape x1, local copies, waits for them, and re-layouts, correlate(): result.reshape(CHANNELS, row_block.shape[3], 2, column_block.shape[3])  12.5 us
  transfers between devices with their start and end apart: 3, of which 3 were waited for; matrix products, arithmetic and copies ran while one was open for 1% of the time, Pallas kernels for 0%

commit v1 on v0

--- a/solution.py
+++ b/solution.py
@@ -9,6 +9,11 @@
 TAPS = 16
 SPECTRA_DEV = 16
 BLOCKS = 2
+
+
+def all_by_exchange(x, axis, d):
+    sent = jnp.stack([x] * lax.axis_size(axis))
+    return jnp.concatenate(lax.all_to_all(sent, axis, 0, 0), axis=d)
 
 
 def from_behind(block, axis, distance):
@@ -83,7 +88,7 @@
     earlier = from_behind(rim_frames, "col", 1)
     extended = jnp.concatenate([earlier, frames], axis=0)
     pieces = channelize(extended, taps, SPECTRA_DEV)
-    row_block = lax.all_gather(pieces, "col", axis=2, tiled=True)
+    row_block = all_by_exchange(pieces, "col", 2)
     ratio = lax.axis_size("row") // lax.axis_size("col")
     first_root = lax.axis_index("col") * ratio
     received = from_root(row_block, "row", first_root + 0)

time: 542 us -> 612 us (1.13)
  waiting for transfers between devices: 461 us -> 508 us
  local copies, waits for them, and re-layouts: 24.7 us -> 36.3 us
  starting transfers between devices: 6.26 us -> 14.4 us
    all_to_all x0 -> x1, waiting for transfers between devices: none -> 131 us  [all_by_exchange(): return jnp.concatenate(lax.all_to_all(sent, axis, 0, 0), axis=d)]
    all_gather x1 -> x0, waiting for transfers between devices: 89.2 us -> none  [body(): row_block = lax.all_gather(pieces, 'col', axis=2, tiled=True)]
    all_to_all x0 -> x1, starting transfers between devices: none -> 8.13 us  [all_by_exchange(): return jnp.concatenate(lax.all_to_all(sent, axis, 0, 0), axis=d)]
    reshape x0 -> x1, local copies, waits for them, and re-layouts: none -> 8.01 us  [all_by_exchange(): return jnp.concatenate(lax.all_to_all(sent, axis, 0, 0), axis=d)]
where the time goes in v1:
time: 612 us; the launch traced here: 611 us
  waiting for transfers between devices  508 us (83%)
  local copies, waits for them, and re-layouts  36.3 us (6%)
  matrix products  27.5 us (4%)
  starting transfers between devices  14.4 us (2%)
  between operations  13.5 us (2%)
  other arithmetic  11.7 us (2%)
    psum x1, waiting for transfers between devices, from_root(): return lax.psum(jnp.where(mine, value, jnp.zeros_like(value)), axis)  366 us
    all_to_all x1, waiting for transfers between devices, all_by_exchange(): return jnp.concatenate(lax.all_to_all(sent, axis, 0, 0), axis=d)  131 us
    dot_general x2, matrix products, correlate(): lax.dot_general(left, right, (((1,), (1,)), ((0,), (0,))), preferred_elem...  22.4 us
    reshape x1, local copies, waits for them, and re-layouts, correlate(): result.reshape(CHANNELS, row_block.shape[3], 2, column_block.shape[3])  12.5 us
  transfers between devices with their start and end apart: 3, of which 3 were waited for; matrix products, arithmetic and copies ran while one was open for 1% of the time, Pallas kernels for 0%

profile of v1, /device:TPU:1, one launch (start us, length us, event | category | flops | bytes accessed | tf_op | source)
XLA Modules:
  0.0 611.5 jit_solution(6307441385178613243)
XLA Ops:
  6.5 0.0 copy-start.1
  6.5 1.8 convert_element_type.72
  8.3 0.1 slice.166
  8.4 6.2 %collective-permute-start = (bf16[15,128,256]{2,1,0:T(8,128)(2,1)S(1)}, bf16[15,128,256]{2,1,0:T(8,128)(2,1)S(1)}, u32[]{:S(2)}, u32[]{:S(2)}) collective-permute-start(bf16[15,128,256]{2,1,0:T(8,128)(2,1)S(1)} %bitcast.63), channel_id=1, source_target_pairs={{0,1},{1,2},{2,3},{3,4},{4,5},{5,6},{6,7},{7,8},{8,9},{9,10},{10,1... | collective-permute-start | bytes 2949128 | tf_op jit(solution)/shard_map/ppermute | solution.py:22
  14.6 0.0 copy-done.1
  14.7 0.2 fusion.128
  14.8 10.8 %collective-permute-done = bf16[15,128,256]{2,1,0:T(8,128)(2,1)S(1)} collective-permute-done((bf16[15,128,256]{2,1,0:T(8,128)(2,1)S(1)}, bf16[15,128,256]{2,1,0:T(8,128)(2,1)S(1)}, u32[]{:S(2)}, u32[]{:S(2)}) %collective-permute-start) | collective-permute-done | bytes 983072 | tf_op jit(solution)/shard_map/ppermute | solution.py:22
  25.6 5.2 fusion.72
  30.8 0.3 copy.6
  31.1 4.3 stack.2
  35.4 8.1 %all-to-all-start = ((bf16[16,2,32,16,256]{4,3,2,1,0:T(8,128)(2,1)}), bf16[16,2,32,16,256]{4,3,2,1,0:T(8,128)(2,1)}, u32[]{:S(2)}, u32[]{:S(2)}) async-start(bf16[16,2,32,16,256]{4,3,2,1,0:T(8,128)(2,1)} %stack.2), calls=%async_computation | async-start | bytes 16777216 | tf_op jit(solution)/shard_map/all_to_all | solution.py:16
  43.6 0.0 all-reduce.2.cloned.1.call-start
  43.6 131.4 %all-to-all-done = bf16[16,2,32,16,256]{4,3,2,1,0:T(8,128)(2,1)} async-done(((bf16[16,2,32,16,256]{4,3,2,1,0:T(8,128)(2,1)}), bf16[16,2,32,16,256]{4,3,2,1,0:T(8,128)(2,1)}, u32[]{:S(2)}, u32[]{:S(2)}) %all-to-all-start) | async-done | bytes 8388640 | tf_op jit(solution)/shard_map/all_to_all | solution.py:16
  175.0 8.0 %copy.7 = bf16[2,32,16,16,256]{4,3,2,1,0:T(8,128)(2,1)} copy(bf16[2,32,16,16,256]{4,3,1,0,2:T(8,128)(2,1)} %bitcast.20) | data formatting | bytes 16777216 | tf_op jit(solution)/shard_map/reshape | solution.py:16
  183.1 7.2 %broadcast_select_fusion = bf16[2,32,256,256]{3,2,1,0:T(8,128)(2,1)} fusion(pred[]{:T(512)S(6)} %eq.5, bf16[2,32,16,16,256]{4,3,2,1,0:T(8,128)(2,1)} %copy.7), kind=kLoop, calls=%fused_computation.16 | loop fusion | flops 4194304 | bytes 16777216 | tf_op jit(solution)/shard_map/jit(_where)/select_n | solution.py:27
  190.2 0.0 all-reduce.2.cloned.1.call-update
  190.2 5.6 slice_bitcast_fusion.3
  195.9 365.8 %all-reduce.2.cloned.1.call-done = bf16[2,32,256,256]{3,2,1,0:T(8,128)(2,1)} async-done(((bf16[2,32,256,256]{3,2,1,0:T(8,128)(2,1)}), bf16[2,32,256,256]{3,2,1,0:T(8,128)(2,1)}) %all-reduce.2.cloned.1.call-update) | async-done | bytes 8388624 | tf_op jit(solution)/shard_map/psum | solution.py:27
  561.7 0.0 copy-start
  561.7 2.6 fusion.134
  564.3 2.0 copy-done
  566.3 3.5 slice_bitcast_fusion
  569.8 10.2 %fusion = f32[32,256,512]{2,1,0:T(8,128)} fusion(bf16[32,128,256]{2,1,0:T(8,128)(2,1)} %get-tuple-element.12, bf16[32,128,256]{2,1,0:T(8,128)(2,1)S(1)} %get-tuple-element.14, bf16[32,128,256]{2,1,0:T(8,128)(2,1)} %get-tuple-element.11, bf16[32,128,256]{2,1,0:T(8,128)(2,1)} %get-tuple-element.7, bf16[32,128,256]{2,1,0:T(8,128)(2,1)} %get-tuple-element.8), kind=kOutput, calls=%fused_computation.1 | convolution fusion | flops 2189426688 | bytes 27262976 | tf_op jit(solution)/shard_map/dot_general | solution.py:73
  580.0 12.1 %multiply_convert_fusion = bf16[32,256,512]{2,1,0:T(8,128)(2,1)} fusion(f32[32,256,512]{2,1,0:T(8,128)} %fusion, bf16[32,128,256]{2,1,0:T(8,128)(2,1)} %get-tuple-element.10, bf16[32,128,256]{2,1,0:T(8,128)(2,1)S(1)} %get-tuple-element.13, bf16[32,128,256]{2,1,0:T(8,128)(2,1)} %get-tuple-element.9, bf16[32,128,256]{2,1,0:T(8,128)(2,1)} %get-tuple-element.6, ...), kind=kOutput, calls=%fused_computation | convolution fusion | flops 2202009600 | bytes 35651584 | tf_op jit(solution)/shard_map/dot_general | solution.py:73
  592.1 12.5 %reshape.41 = bf16[32,256,2,256]{3,2,1,0:T(2,128)(2,1)} reshape(bf16[32,256,512]{2,1,0:T(8,128)(2,1)} %multiply_convert_fusion) | data formatting | bytes 16777216 | tf_op jit(solution)/shard_map/reshape | solution.py:82
  (3 shorter events, 0.0 us)
Async XLA Ops:
  6.5 8.1 %copy-start.1 = (s32[16,128]{1,0:T(8,128)S(1)}, s32[16,128]{1,0:T(8,128)}, u32[]{:S(2)}) copy-start(s32[16,128]{1,0:T(8,128)} %param.3) | copy-start | bytes 24580
  8.4 17.2 %collective-permute-start = (bf16[15,128,256]{2,1,0:T(8,128)(2,1)S(1)}, bf16[15,128,256]{2,1,0:T(8,128)(2,1)S(1)}, u32[]{:S(2)}, u32[]{:S(2)}) collective-permute-start(bf16[15,128,256]{2,1,0:T(8,128)(2,1)S(1)} %bitcast.63), channel_id=1, source_target_pairs={{0,1},{1,2},{2,3},{3,4},{4,5},{5,6},{6,7},{7,8},{8,9},{9,10},{10,1... | collective-permute-start | bytes 2949128 | tf_op jit(solution)/shard_map/ppermute | solution.py:22
  35.4 139.6 %all-to-all-start = ((bf16[16,2,32,16,256]{4,3,2,1,0:T(8,128)(2,1)}), bf16[16,2,32,16,256]{4,3,2,1,0:T(8,128)(2,1)}, u32[]{:S(2)}, u32[]{:S(2)}) async-start(bf16[16,2,32,16,256]{4,3,2,1,0:T(8,128)(2,1)} %stack.2), calls=%async_computation | async-start | bytes 16777216 | tf_op jit(solution)/shard_map/all_to_all | solution.py:16
  43.6 518.1 %all-reduce.2.cloned.1.call-start = ((), (), s32[]{:S(2)}) async-start(), calls=%async_computation.1 | async-start | bytes 16777216 | tf_op jit(solution)/shard_map/psum | solution.py:27
  561.7 4.6 copy-start
Sparse Core Ops, SparseCore 0:
  190.4 371.2 all-reduce.1
